TPU v7x, 32 devices: a whole 2x2x4 slice. The times are simulated.
32 devices in a mesh: groups: 2 (over y), blk: 4 (over z), dp: 2 (over x), sub: 2 (over core).
Axes of the slice: x: 2, y: 2, z: 4, core: 2. Of those that a mesh axis runs over, the one named last changes fastest.
Arguments:
- view_a: bfloat16 [2048, 256], P(('groups', 'blk', 'dp', 'sub')), parts along dimension 0, may hold values from -6 to 6
- view_b: bfloat16 [2048, 256], P(('groups', 'blk', 'dp', 'sub')), parts along dimension 0, may hold values from -6 to 6
- prototypes: bfloat16 [32768, 256], P('blk'), may hold values from -6 to 6
- tile_mask: int32 [16, 256], replicated, may hold values from 0 to 1, as said below
- tile_region: int32 [32], P('groups'), parts along dimension 0, may hold values from 0 to 15, as said below
Outputs:
- grad_view_b: float32 [2048, 256], P(('groups', 'blk', 'dp', 'sub')), parts along dimension 0
- grad_prototypes: float32 [65536, 256], P(('groups', 'blk', 'dp', 'sub')), parts along dimension 0
There are 2 independent parts, one for each index of `groups`. A program takes and returns all parts, laid end to end along the dimension named above; an argument that names none is the same for every part. Nothing has to cross between parts.
Inputs may be any that keep to these rules, and one draw needn't show every extreme that they name: `tile_mask`: every prototype tile is 1 for at least one region, and every region for at least 16 tiles. `tile_region`: every region is named by at least one hit tile.
All inputs are finite; a program needn't handle non-finite values.
Results may differ from a plain program's by a relative error of at most 0.00045.
The roundings to bfloat16 on the way count: a program that leaves them out, or rounds other values in their place, can miss the bound.
Values may be sent and summed in bfloat16 or wider, within the bound.
A program may use at most 64 MiB of HBM per device.

v0:
```python
import jax
import jax.numpy as jnp
from jax import lax
from jax.sharding import PartitionSpec as P

TILE = 128
ITERS = 3


SOFTMAX_TEMPER = 0.1
EPSILON = 0.05


def from_behind(block, axis, distance):
    devices = range(lax.axis_size(axis))
    route = [((i - distance) % len(devices), i) for i in devices]
    return lax.ppermute(block, axis, route)


def unit_rows(matrix):
    values = matrix.astype(jnp.float32)
    return (values * lax.rsqrt(jnp.sum(values * values, axis=1, keepdims=True) + 1e-06)).astype(
        jnp.bfloat16
    )


def to_global(vector, blk_pos, block_count):
    return jnp.roll(vector[::-1], blk_pos + 1 - block_count, axis=0)


def body(view_a, view_b, prototypes, tile_mask, tile_region):
    n_blk = lax.axis_size("blk")
    n_dp = lax.axis_size("dp")
    n_sub = lax.axis_size("sub")
    blk_pos = lax.axis_index("blk")
    dp_pos = lax.axis_index("dp")
    sub_pos = lax.axis_index("sub")
    hit_dev = view_a.shape[0]
    block_rows = prototypes.shape[0]
    share_cols = block_rows // n_dp
    tiles_share = share_cols // TILE
    tiles_block = block_rows // TILE
    regions = tile_mask.shape[0]
    own_block = unit_rows(lax.dynamic_slice_in_dim(prototypes, dp_pos * share_cols, share_cols, 0))
    unit_a = unit_rows(view_a)
    unit_b = unit_rows(view_b)
    rows_a, rows_b = (
        lax.all_gather(unit_a, "dp", axis=0, tiled=True),
        lax.all_gather(unit_b, "dp", axis=0, tiled=True),
    )
    detector_hit_rows = rows_a.shape[0]
    both_rows = jnp.concatenate([rows_a, rows_b], axis=0)
    region_grid = tile_region.reshape(n_blk, n_dp, n_sub)
    my_regions = lax.dynamic_index_in_dim(
        lax.dynamic_index_in_dim(region_grid, blk_pos, 0, keepdims=False),
        sub_pos,
        1,
        keepdims=False,
    )
    onehot = (my_regions[:, None] == jnp.arange(regions, dtype=jnp.int32)[None, :]).astype(
        jnp.float32
    )
    row_tiles = jnp.dot(onehot, tile_mask.astype(jnp.float32))

    def active_at(block_id):
        tile_flags = lax.dynamic_slice_in_dim(
            row_tiles, block_id * tiles_block + dp_pos * tiles_share, tiles_share, 1
        )
        expanded = jnp.broadcast_to(
            tile_flags[:, None, :, None] > 0.5, (n_dp, hit_dev, tiles_share, TILE)
        )
        return expanded.reshape(detector_hit_rows, share_cols)

    def forward(proto_block, block_id):
        prototype_scores = jnp.einsum(
            "rd,kd->rk", both_rows, proto_block, preferred_element_type=jnp.float32
        )
        live_block_mask = active_at(block_id)
        code_exp = jnp.where(
            live_block_mask, jnp.exp((prototype_scores[:detector_hit_rows] - 1.0) / EPSILON), 0.0
        ).astype(jnp.bfloat16)
        prototype_weights = jnp.where(
            live_block_mask,
            jnp.exp((prototype_scores[detector_hit_rows:] - 1.0) / SOFTMAX_TEMPER),
            0.0,
        )
        return (
            code_exp,
            jnp.sum(code_exp.astype(jnp.float32), axis=0),
            jnp.sum(prototype_weights, axis=1),
        )

    code_first, colsum_first, norm_first = forward(own_block, blk_pos)
    code_stack = (
        jnp.zeros((n_blk, detector_hit_rows, share_cols), jnp.bfloat16).at[0].set(code_first)
    )
    colsum_stack = jnp.zeros((n_blk, share_cols), jnp.float32).at[0].set(colsum_first)
    block_stack = jnp.zeros((1,), jnp.bfloat16)

    def forward_turn(carry_state, turn_index):
        proto_block, code_all, colsum_all, blocks_all, norm_part = carry_state
        proto_block = from_behind(proto_block, "blk", 1)
        block_id = (blk_pos - turn_index) % n_blk
        code_exp, colsum, norm_add = forward(proto_block, block_id)
        code_all = lax.dynamic_update_index_in_dim(code_all, code_exp, turn_index, 0)
        colsum_all = lax.dynamic_update_index_in_dim(colsum_all, colsum, turn_index, 0)
        return ((proto_block, code_all, colsum_all, blocks_all, norm_part + norm_add), None)

    turns = jnp.arange(1, n_blk, dtype=jnp.int32)
    carry_state, unused = lax.scan(
        forward_turn, (own_block, code_stack, colsum_stack, block_stack, norm_first), turns
    )
    code_all = carry_state[1]
    colsum_all = carry_state[2]
    blocks_all = carry_state[3]
    norm_part = carry_state[4]

    def column_recip(colsum_steps):
        global_sums = to_global(colsum_steps, blk_pos, n_blk).reshape(-1)
        totals = lax.psum(global_sums, ("blk", "sub"))
        recip_vec = 1.0 / totals
        return to_global(recip_vec.reshape(n_blk, share_cols), blk_pos, n_blk)

    def row_partial(column_inverses):
        return jnp.sum(code_all.astype(jnp.float32) * column_inverses[:, None, :], axis=(0, 2))

    column_inverses = column_recip(colsum_all)
    row_totals, second_view_norm = lax.psum((row_partial(column_inverses), norm_part), "dp")
    row_inverses = 1.0 / row_totals
    for sweep_index in range(ITERS - 1):
        colsum_all = jnp.sum(code_all.astype(jnp.float32) * row_inverses[None, :, None], axis=1)
        column_inverses = column_recip(colsum_all)
        row_inverses = 1.0 / lax.psum(row_partial(column_inverses), "dp")

    def backward(proto_block, turn_index, block_id):
        prototype_scores = jnp.einsum(
            "rd,kd->rk", rows_b, proto_block, preferred_element_type=jnp.float32
        )
        live_block_mask = active_at(block_id)
        predicted_logits = (
            jnp.where(live_block_mask, jnp.exp((prototype_scores - 1.0) / SOFTMAX_TEMPER), 0.0)
            / second_view_norm[:, None]
        )
        code_exp = lax.dynamic_index_in_dim(code_all, turn_index, 0, keepdims=False).astype(
            jnp.float32
        )
        col_vals = lax.dynamic_index_in_dim(column_inverses, turn_index, 0, keepdims=False)
        code_entries = row_inverses[:, None] * code_exp * col_vals[None, :]
        score_gradient = ((predicted_logits - code_entries) / SOFTMAX_TEMPER).astype(jnp.bfloat16)
        hit_part = jnp.dot(score_gradient, proto_block, preferred_element_type=jnp.float32)
        proto_part = jnp.einsum(
            "rk,rd->kd", score_gradient, rows_b, preferred_element_type=jnp.float32
        )
        return (hit_part, proto_part)

    def pass_grads(running):
        return from_behind(running, "blk", 1)

    hit_first, proto_first = backward(own_block, 0, blk_pos)

    def backward_turn(carry_state, turn_index):
        proto_block, hit_running, proto_running = carry_state
        block_id = (blk_pos - turn_index) % n_blk
        proto_block = from_behind(proto_block, "blk", 1)
        proto_running = pass_grads(proto_running)
        hit_part, proto_part = backward(proto_block, turn_index, block_id)
        return ((proto_block, hit_running + hit_part, proto_running + proto_part), None)

    carry_state, unused = lax.scan(backward_turn, (own_block, hit_first, proto_first), turns)
    proto_home = pass_grads(carry_state[2])
    grad_view_b = lax.psum_scatter(carry_state[1], "dp", scatter_dimension=0, tiled=True)
    grad_prototypes = lax.psum_scatter(proto_home, "sub", scatter_dimension=0, tiled=True)
    return (grad_view_b, grad_prototypes)


def solution(mesh):
    placed = (
        P(("groups", "blk", "dp", "sub"), None),
        P(("groups", "blk", "dp", "sub"), None),
        P("blk", None),
        P(),
        P("groups"),
    )
    return jax.shard_map(
        body,
        mesh=mesh,
        in_specs=placed,
        out_specs=(
            P(("groups", "blk", "dp", "sub"), None),
            P(("groups", "blk", "dp", "sub"), None),
        ),
        check_vma=False,
    )
```

profile of v0, /device:TPU:0, one launch (start us, length us, event | category | flops | bytes accessed | tf_op | source)
XLA Modules:
  0.0 934.0 jit_solution(10555834925362059622)
XLA Ops:
  12.4 5.5 all_gather.6
  18.1 4.6 all_gather.7
  24.1 2.7 fusion.61
  27.5 3.4 fusion.33
  33.3 155.7 %while.37 = (s32[]{:T(128)}, bf16[4096,256]{1,0:T(8,128)(2,1)}, bf16[4,128,4096]{2,1,0:T(8,128)(2,1)}, f32[4,4096]{1,0:T(4,128)S(1)}, f32[128]{0:T(128)S(1)}, /*...) while((s32[]{:T(128)}, bf16[4096,256]{1,0:T(8,128)(2,1)}, ...), condition=%wide.region_8.9_spmd, body=%wide.region_5.8_spmd.sunk | while | flops 544206912 | bytes 27970340 | solution.py:110
  38.9 42.1 %collective-permute-done = bf16[4096,256]{1,0:T(8,128)(2,1)S(1)} collective-permute-done((bf16[4096,256]{1,0:T(8,128)(2,1)}, bf16[4096,256]{1,0:T(8,128)(2,1)S(1)}, u32[]{:S(2)}, u32[]{:S(2)}) %collective-permute-start) | collective-permute-done | bytes 2097184 | tf_op jit(solution)/shard_map/while/body/eval_jaxpr/ppermute | solution.py:17
  89.8 43.0 %collective-permute-done = bf16[4096,256]{1,0:T(8,128)(2,1)S(1)} collective-permute-done((bf16[4096,256]{1,0:T(8,128)(2,1)}, bf16[4096,256]{1,0:T(8,128)(2,1)S(1)}, u32[]{:S(2)}, u32[]{:S(2)}) %collective-permute-start) | collective-permute-done | bytes 2097184 | tf_op jit(solution)/shard_map/while/body/eval_jaxpr/ppermute | solution.py:17
  141.6 42.1 %collective-permute-done = bf16[4096,256]{1,0:T(8,128)(2,1)S(1)} collective-permute-done((bf16[4096,256]{1,0:T(8,128)(2,1)}, bf16[4096,256]{1,0:T(8,128)(2,1)S(1)}, u32[]{:S(2)}, u32[]{:S(2)}) %collective-permute-start) | collective-permute-done | bytes 2097184 | tf_op jit(solution)/shard_map/while/body/eval_jaxpr/ppermute | solution.py:17
  190.5 51.5 %all-reduce.7.cloned.1.call-done = f32[16384]{0:T(1024)} async-done(((f32[16384]{0:T(1024)}), f32[16384]{0:T(1024)}) %all-reduce.7.cloned.1.call-update) | async-done | bytes 65552 | tf_op jit(solution)/shard_map/psum | solution.py:120
  243.8 3.1 fusion.16
  246.9 4.9 psum.51
  251.8 3.2 fusion.17
  256.6 52.7 %all-reduce.9.cloned.1.call-done = f32[16384]{0:T(1024)} async-done(((f32[16384]{0:T(1024)}), f32[16384]{0:T(1024)}) %all-reduce.9.cloned.1.call-update) | async-done | bytes 65552 | tf_op jit(solution)/shard_map/psum | solution.py:120
  311.1 3.1 fusion.18
  314.2 4.9 psum.53
  319.1 3.2 fusion.19
  324.1 52.5 %all-reduce.11.cloned.1.call-done = f32[16384]{0:T(1024)} async-done(((f32[16384]{0:T(1024)}), f32[16384]{0:T(1024)}) %all-reduce.11.cloned.1.call-update) | async-done | bytes 65552 | tf_op jit(solution)/shard_map/psum | solution.py:120
  378.4 3.2 fusion.20
  381.6 4.9 all-reduce.2
  386.6 2.5 fusion.27
  389.1 2.7 fusion.63
  392.3 435.9 %while.38 = (s32[]{:T(128)}, bf16[4096,256]{1,0:T(8,128)(2,1)S(1)}, f32[128,256]{1,0:T(8,128)S(1)}, f32[4096,256]{1,0:T(8,128)}, s32[3]{0:T(128)S(1)}, /*index=5...) while((s32[]{:T(128)}, bf16[4096,256]{1,0:T(8,128)(2,1)S(1)}, ...), condition=%wide.region_22.24_spmd, body=%wide.region_21.23_spmd.sunk | while | flops 811630720 | bytes 64407448 | solution.py:169
  397.7 131.2 %collective-permute-done.1 = bf16[4096,256]{1,0:T(8,128)(2,1)S(1)} collective-permute-done((bf16[4096,256]{1,0:T(8,128)(2,1)}, bf16[4096,256]{1,0:T(8,128)(2,1)S(1)}, u32[]{:S(2)}, u32[]{:S(2)}) %collective-permute-start.1) | collective-permute-done | bytes 2097184 | tf_op jit(solution)/shard_map/while/body/eval_jaxpr/ppermute | solution.py:17
  533.5 5.1 convolution_add_fusion.7
  543.2 131.0 %collective-permute-done.1 = bf16[4096,256]{1,0:T(8,128)(2,1)S(1)} collective-permute-done((bf16[4096,256]{1,0:T(8,128)(2,1)}, bf16[4096,256]{1,0:T(8,128)(2,1)S(1)}, u32[]{:S(2)}, u32[]{:S(2)}) %collective-permute-start.1) | collective-permute-done | bytes 2097184 | tf_op jit(solution)/shard_map/while/body/eval_jaxpr/ppermute | solution.py:17
  675.7 2.5 fusion.101
  678.8 5.1 convolution_add_fusion.7
  688.5 130.1 %collective-permute-done.1 = bf16[4096,256]{1,0:T(8,128)(2,1)S(1)} collective-permute-done((bf16[4096,256]{1,0:T(8,128)(2,1)}, bf16[4096,256]{1,0:T(8,128)(2,1)S(1)}, u32[]{:S(2)}, u32[]{:S(2)}) %collective-permute-start.1) | collective-permute-done | bytes 2097184 | tf_op jit(solution)/shard_map/while/body/eval_jaxpr/ppermute | solution.py:17
  820.1 2.5 fusion.101
  823.1 5.1 convolution_add_fusion.7
  828.9 88.2 %collective-permute-done.3 = f32[4096,256]{1,0:T(8,128)} collective-permute-done((f32[4096,256]{1,0:T(8,128)}, f32[4096,256]{1,0:T(8,128)}, u32[]{:S(2)}, u32[]{:S(2)}) %collective-permute-start.3) | collective-permute-done | bytes 4194336 | tf_op jit(solution)/shard_map/ppermute | solution.py:17
  917.2 10.3 %reduce-scatter.5.cloned.1.call-done = f32[2048,256]{1,0:T(8,128)} async-done(((f32[4096,256]{1,0:T(8,128)}), f32[2048,256]{1,0:T(8,128)}) %reduce-scatter.5.cloned.1.call-update) | async-done | bytes 2097168 | tf_op jit(solution)/shard_map/reduce_scatter | solution.py:172
  (140 shorter events, 56.6 us)
Async XLA Ops:
  7.2 234.9 %all-reduce.7.cloned.1.call-start = ((), (), s32[]{:S(2)}) async-start(), calls=%async_computation.2 | async-start | bytes 131072 | tf_op jit(solution)/shard_map/psum | solution.py:120
  10.2 2.0 copy-start.5
  10.2 7.7 copy-start.6
  12.2 11.9 %copy-start = (bf16[4096,256]{1,0:T(8,128)(2,1)}, bf16[4096,256]{1,0:T(8,128)(2,1)S(1)}, u32[]{:S(2)}) copy-start(bf16[4096,256]{1,0:T(8,128)(2,1)S(1)} %fusion.29) | copy-start | bytes 6291460
  24.1 2.9 copy-start.7
  33.3 47.7 %collective-permute-start = (bf16[4096,256]{1,0:T(8,128)(2,1)}, bf16[4096,256]{1,0:T(8,128)(2,1)S(1)}, u32[]{:S(2)}, u32[]{:S(2)}) collective-permute-start(bf16[4096,256]{1,0:T(8,128)(2,1)} %get-tuple-element.575), channel_id=1, source_target_pairs={{12,0},{0,4},{4,8},{8,12},{13,1},{1,5},{5,9},{9,13},{14,2},{2,6},{... | collective-permute-start | bytes 6291464 | tf_op jit(solution)/shard_map/while/body/eval_jaxpr/ppermute | solution.py:17
  86.4 46.4 %collective-permute-start = (bf16[4096,256]{1,0:T(8,128)(2,1)}, bf16[4096,256]{1,0:T(8,128)(2,1)S(1)}, u32[]{:S(2)}, u32[]{:S(2)}) collective-permute-start(bf16[4096,256]{1,0:T(8,128)(2,1)} %get-tuple-element.575), channel_id=1, source_target_pairs={{12,0},{0,4},{4,8},{8,12},{13,1},{1,5},{5,9},{9,13},{14,2},{2,6},{... | collective-permute-start | bytes 6291464 | tf_op jit(solution)/shard_map/while/body/eval_jaxpr/ppermute | solution.py:17
  138.2 45.5 %collective-permute-start = (bf16[4096,256]{1,0:T(8,128)(2,1)}, bf16[4096,256]{1,0:T(8,128)(2,1)S(1)}, u32[]{:S(2)}, u32[]{:S(2)}) collective-permute-start(bf16[4096,256]{1,0:T(8,128)(2,1)} %get-tuple-element.575), channel_id=1, source_target_pairs={{12,0},{0,4},{4,8},{8,12},{13,1},{1,5},{5,9},{9,13},{14,2},{2,6},{... | collective-permute-start | bytes 6291464 | tf_op jit(solution)/shard_map/while/body/eval_jaxpr/ppermute | solution.py:17
  190.5 118.8 %all-reduce.9.cloned.1.call-start = ((), (), s32[]{:S(2)}) async-start(), calls=%async_computation.3 | async-start | bytes 131072 | tf_op jit(solution)/shard_map/psum | solution.py:120
  256.6 120.0 %all-reduce.11.cloned.1.call-start = ((), (), s32[]{:S(2)}) async-start(), calls=%async_computation.4 | async-start | bytes 131072 | tf_op jit(solution)/shard_map/psum | solution.py:120
  323.9 593.3 %reduce-scatter.3.cloned.1.call-start = ((), (), s32[]{:S(2)}) async-start(), calls=%async_computation.5 | async-start | bytes 196608 | tf_op jit(solution)/shard_map/reduce_scatter | solution.py:171
  378.4 8.2 copy-start.1
  392.3 1.3 copy-start.2
  392.4 141.1 %collective-permute-start.2 = (f32[4096,256]{1,0:T(8,128)}, f32[4096,256]{1,0:T(8,128)}, u32[]{:S(2)}, u32[]{:S(2)}) collective-permute-start(f32[4096,256]{1,0:T(8,128)} %get-tuple-element.628), channel_id=1, source_target_pairs={{12,0},{0,4},{4,8},{8,12},{13,1},{1,5},{5,9},{9,13},{14,2},{2,6},{... | collective-permute-start | bytes 12582920 | tf_op jit(solution)/shard_map/while/body/eval_jaxpr/ppermute | solution.py:17
  393.7 135.3 %collective-permute-start.1 = (bf16[4096,256]{1,0:T(8,128)(2,1)}, bf16[4096,256]{1,0:T(8,128)(2,1)S(1)}, u32[]{:S(2)}, u32[]{:S(2)}) collective-permute-start(bf16[4096,256]{1,0:T(8,128)(2,1)} %copy-done.2), channel_id=1, source_target_pairs={{12,0},{0,4},{4,8},{8,12},{13,1},{1,5},{5,9},{9,13},{14,2},{2,6},{... | collective-permute-start | bytes 6291464 | tf_op jit(solution)/shard_map/while/body/eval_jaxpr/ppermute | solution.py:17
  533.5 5.1 copy-start.3
  538.6 1.3 copy-start.2
  538.6 140.2 %collective-permute-start.2 = (f32[4096,256]{1,0:T(8,128)}, f32[4096,256]{1,0:T(8,128)}, u32[]{:S(2)}, u32[]{:S(2)}) collective-permute-start(f32[4096,256]{1,0:T(8,128)} %get-tuple-element.628), channel_id=1, source_target_pairs={{12,0},{0,4},{4,8},{8,12},{13,1},{1,5},{5,9},{9,13},{14,2},{2,6},{... | collective-permute-start | bytes 12582920 | tf_op jit(solution)/shard_map/while/body/eval_jaxpr/ppermute | solution.py:17
  539.9 134.3 %collective-permute-start.1 = (bf16[4096,256]{1,0:T(8,128)(2,1)}, bf16[4096,256]{1,0:T(8,128)(2,1)S(1)}, u32[]{:S(2)}, u32[]{:S(2)}) collective-permute-start(bf16[4096,256]{1,0:T(8,128)(2,1)} %copy-done.2), channel_id=1, source_target_pairs={{12,0},{0,4},{4,8},{8,12},{13,1},{1,5},{5,9},{9,13},{14,2},{2,6},{... | collective-permute-start | bytes 6291464 | tf_op jit(solution)/shard_map/while/body/eval_jaxpr/ppermute | solution.py:17
  678.8 5.1 copy-start.3
  683.9 1.3 copy-start.2
  683.9 139.2 %collective-permute-start.2 = (f32[4096,256]{1,0:T(8,128)}, f32[4096,256]{1,0:T(8,128)}, u32[]{:S(2)}, u32[]{:S(2)}) collective-permute-start(f32[4096,256]{1,0:T(8,128)} %get-tuple-element.628), channel_id=1, source_target_pairs={{12,0},{0,4},{4,8},{8,12},{13,1},{1,5},{5,9},{9,13},{14,2},{2,6},{... | collective-permute-start | bytes 12582920 | tf_op jit(solution)/shard_map/while/body/eval_jaxpr/ppermute | solution.py:17
  685.2 133.4 %collective-permute-start.1 = (bf16[4096,256]{1,0:T(8,128)(2,1)}, bf16[4096,256]{1,0:T(8,128)(2,1)S(1)}, u32[]{:S(2)}, u32[]{:S(2)}) collective-permute-start(bf16[4096,256]{1,0:T(8,128)(2,1)} %copy-done.2), channel_id=1, source_target_pairs={{12,0},{0,4},{4,8},{8,12},{13,1},{1,5},{5,9},{9,13},{14,2},{2,6},{... | collective-permute-start | bytes 6291464 | tf_op jit(solution)/shard_map/while/body/eval_jaxpr/ppermute | solution.py:17
  823.1 5.1 copy-start.3
  828.2 0.6 copy-start.4
  828.2 88.9 %collective-permute-start.3 = (f32[4096,256]{1,0:T(8,128)}, f32[4096,256]{1,0:T(8,128)}, u32[]{:S(2)}, u32[]{:S(2)}) collective-permute-start(f32[4096,256]{1,0:T(8,128)} %get-tuple-element.360), channel_id=1, source_target_pairs={{12,0},{0,4},{4,8},{8,12},{13,1},{1,5},{5,9},{9,13},{14,2},{2,6},{... | collective-permute-start | bytes 12582920 | tf_op jit(solution)/shard_map/ppermute | solution.py:17
  828.9 98.6 %reduce-scatter.5.cloned.1.call-start = ((), (), s32[]{:S(2)}) async-start(), calls=%async_computation.6 | async-start | bytes 6291456 | tf_op jit(solution)/shard_map/reduce_scatter | solution.py:172
Sparse Core Ops, SparseCore 0:
  190.6 51.3 all-reduce.6
  256.7 52.5 all-reduce.8
  324.0 52.5 all-reduce.10
  829.0 11.0 reduce-scatter.2
  917.3 10.2 reduce-scatter.4
where the time goes:
time: 935 us; the launch traced here: 934 us
  waiting for transfers between devices  775 us (83%)
  other arithmetic  35.5 us (4%)
  matrix products  35.1 us (4%)
  local copies, waits for them, and re-layouts  29.5 us (3%)
  blocking collectives  24.9 us (3%)
  loops' own time  16.2 us (2%)
  between operations  14.1 us (2%)
    ppermute x10, waiting for transfers between devices, from_behind(): return lax.ppermute(block, axis, route)  608 us
    psum x3, waiting for transfers between devices, column_recip(): totals = lax.psum(global_sums, ('blk', 'sub'))  157 us
  transfers between devices with their start and end apart: 15, of which 11 were waited for; matrix products, arithmetic and copies ran while one was open for 2% of the time, Pallas kernels for 0%

commit v1 on v0

v1 whole, which is shorter than its diff:
```python
import jax
import jax.numpy as jnp
from jax import lax
from jax.sharding import PartitionSpec as P

TILE = 128
ITERS = 3
SOFTMAX_TEMPER = 0.1
EPSILON = 0.05
PART = ("blk", "dp", "sub")


def unit_rows(matrix):
    values = matrix.astype(jnp.float32)
    return (values * lax.rsqrt(jnp.sum(values * values, axis=1, keepdims=True) + 1e-06)).astype(
        jnp.bfloat16
    )


def body(view_a, view_b, prototypes, tile_mask, tile_region):
    n_dp = lax.axis_size("dp")
    n_sub = lax.axis_size("sub")
    blk_pos = lax.axis_index("blk")
    inner_pos = lax.axis_index("dp") * n_sub + lax.axis_index("sub")
    hit_dev, width = view_a.shape
    cols = prototypes.shape[0] // (n_dp * n_sub)
    tiles = cols // TILE
    regions = tile_mask.shape[0]
    protos = unit_rows(lax.dynamic_slice_in_dim(prototypes, inner_pos * cols, cols, 0))
    both = jnp.concatenate([unit_rows(view_a), unit_rows(view_b)], axis=1)
    both = lax.all_gather(both, PART, axis=0, tiled=True)
    rows_a, rows_b = both[:, :width], both[:, width:]
    hits = rows_a.shape[0]
    own_tile = (blk_pos * n_dp * n_sub + inner_pos) * tiles
    my_mask = lax.dynamic_slice_in_dim(tile_mask, own_tile, tiles, 1).astype(jnp.float32)
    onehot = (tile_region[:, None] == jnp.arange(regions, dtype=jnp.int32)[None, :]).astype(
        jnp.float32
    )
    flags = jnp.dot(onehot, my_mask) > 0.5
    active = jnp.broadcast_to(
        flags[:, None, :, None], (hits // hit_dev, hit_dev, tiles, TILE)
    ).reshape(hits, cols)

    def scores(rows):
        return jnp.einsum("rd,kd->rk", rows, protos, preferred_element_type=jnp.float32)

    code_exp = jnp.where(active, jnp.exp((scores(rows_a) - 1.0) / EPSILON), 0.0).astype(
        jnp.bfloat16
    )
    pred = jnp.where(active, jnp.exp((scores(rows_b) - 1.0) / SOFTMAX_TEMPER), 0.0)
    norm = jnp.sum(pred, axis=1)
    code = code_exp.astype(jnp.float32)
    row = jnp.ones((hits,), jnp.float32)
    for sweep in range(ITERS):
        col = 1.0 / jnp.sum(code * row[:, None], axis=0)
        part = jnp.sum(code * col[None, :], axis=1)
        if sweep == 0:
            part, norm = lax.psum((part, norm), PART)
        else:
            part = lax.psum(part, PART)
        row = 1.0 / part
    grad = (
        (pred / norm[:, None] - row[:, None] * code * col[None, :]) / SOFTMAX_TEMPER
    ).astype(jnp.bfloat16)
    hit_part = jnp.dot(grad, protos, preferred_element_type=jnp.float32)
    grad_protos = jnp.einsum("rk,rd->kd", grad, rows_b, preferred_element_type=jnp.float32)
    return (lax.psum_scatter(hit_part, PART, scatter_dimension=0, tiled=True), grad_protos)


def solution(mesh):
    spread = P(("groups", "blk", "dp", "sub"), None)
    return jax.shard_map(
        body,
        mesh=mesh,
        in_specs=(spread, spread, P("blk", None), P(), P("groups")),
        out_specs=(spread, spread),
        check_vma=False,
    )
```

time: 935 us -> 245 us (0.26)
  waiting for transfers between devices: 775 us -> 88.3 us
  blocking collectives: 24.9 us -> 91.2 us
  local copies, waits for them, and re-layouts: 29.5 us -> 4.48 us
  loops' own time: 16.2 us -> 0 us
  matrix products: 35.1 us -> 20.9 us
  other arithmetic: 35.5 us -> 25.6 us
    ppermute x10 -> x0, waiting for transfers between devices: 608 us -> none  [from_behind(): return lax.ppermute(block, axis, route)]
    psum x3 -> x0, waiting for transfers between devices: 157 us -> none  [column_recip(): totals = lax.psum(global_sums, ('blk', 'sub'))]
    psum x3, blocking collectives: 14.8 us -> 91.2 us  [the longest x2 59.6 us: body(): part = lax.psum(part, PART)]
    reduce_scatter x2 -> x1, waiting for transfers between devices: 10.4 us -> 49.9 us  [body(): lax.psum_scatter(hit_part, PART, scatter_dimension=0, tiled=True)]
    all_gather x0 -> x1, waiting for transfers between devices: none -> 38.3 us  [body(): both = lax.all_gather(both, PART, axis=0, tiled=True)]
    another operation x2 -> x0, loops' own time: 16.2 us -> none  [the longest x1 8.21 us: body(): lax.scan(forward_turn, (own_block, code_stack, colsum_stack, block_stack,...]
    dot_general x17 -> x5, matrix products: 35.1 us -> 20.9 us  [the longest x2 11.6 us: scores(): jnp.einsum('rd,kd->rk', rows, protos, preferred_element_type=jnp.float32)]
    while x18 -> x0, local copies, waits for them, and re-layouts: 11.5 us -> none
  transfers between devices with their start and end apart: 15 -> 2, of which waited for: 11 -> 2; matrix products, arithmetic and copies ran while one was open for 2% -> 3% of each run, Pallas kernels for 0% -> 0%
where the time goes in v1:
time: 245 us
  blocking collectives  91.2 us (37%)
  waiting for transfers between devices  88.3 us (36%)
  other arithmetic  25.6 us (10%)
  matrix products  20.9 us (9%)
  between operations  14.2 us (6%)
  local copies, waits for them, and re-layouts  4.48 us (2%)
    psum x2, blocking collectives, body(): part = lax.psum(part, PART)  59.6 us
    reduce_scatter x1, waiting for transfers between devices, body(): lax.psum_scatter(hit_part, PART, scatter_dimension=0, tiled=True)  49.9 us
    all_gather x1, waiting for transfers between devices, body(): both = lax.all_gather(both, PART, axis=0, tiled=True)  38.3 us
    psum x1, blocking collectives, body(): part, norm = lax.psum((part, norm), PART)  31.6 us
    dot_general x2, matrix products, scores(): jnp.einsum('rd,kd->rk', rows, protos, preferred_element_type=jnp.float32)  11.6 us
    convert_element_type x1, other arithmetic, body(): grad = ((pred / norm[:, None] - row[:, None] * code * col[None, :]) / SOF...  7.44 us
    reduce_sum x3, other arithmetic, body(): part = jnp.sum(code * col[None, :], axis=1)  7.06 us
    reduce_sum x2, other arithmetic, body(): col = 1.0 / jnp.sum(code * row[:, None], axis=0)  6.24 us
  transfers between devices with their start and end apart: 2, of which 2 were waited for; matrix products, arithmetic and copies ran while one was open for 3% of the time, Pallas kernels for 0%

profile of v1, /device:TPU:0, one launch (start us, length us, event | category | flops | bytes accessed | tf_op | source)
XLA Modules:
  0.0 244.8 jit_solution(6231227928295905269)
XLA Ops:
  7.2 0.0 all-gather.2.cloned.1.call-start
  7.2 0.9 fusion.17
  8.1 0.9 fusion.19
  9.0 0.9 fusion.18
  9.9 0.6 pad_maximum_fusion
  10.5 0.0 all-gather.2.cloned.1.call-update
  10.5 0.0 reduce-scatter.2.cloned.1.call-start
  10.6 1.6 fusion.10
  12.2 0.9 convolution_compare_fusion
  13.1 38.3 %all-gather.2.cloned.1.call-done = bf16[1024,512]{1,0:T(8,128)(2,1)} async-done(((bf16[64,512]{1,0:T(8,128)(2,1)}), bf16[1024,512]{1,0:T(8,128)(2,1)}) %all-gather.2.cloned.1.call-update) | async-done | bytes 1048592 | tf_op jit(solution)/shard_map/all_gather | solution.py:31
  51.4 0.6 broadcast_in_dim.6
  52.0 4.3 %convert_reduce_fusion = (f32[2048]{0:T(1024)S(1)}, bf16[1024,2048]{1,0:T(8,128)(2,1)S(1)}) fusion(f32[2048]{0:T(1024)S(1)} %add_rsqrt_fusion, bf16[8192,256]{1,0:T(8,128)(2,1)} %param.7, s32[]{:T(128)S(6)} %select_n.14, bf16[1024,512]{1,0:T(8,128)(2,1)} %all-gather.2.cloned.1.call-done, pred[128,8,16,128]{3,2,1,0:T(8,128)(4,1)S(1)} %bitcast.11), kind=kOutput, calls=%fused_computation.6 | convolution fusion | flops 1087895552 | bytes 7880708 | tf_op jit(solution)/shard_map/rd,kd->rk/dot_general | solution.py:45
  56.3 0.0 copy-start
  56.4 2.0 copy-done
  58.3 0.9 fusion
  59.2 31.6 %psum.29 = f32[1024]{0:T(1024)S(1)} all-reduce(f32[1024]{0:T(1024)S(1)} %fusion), channel_id=1, replica_groups=mesh['groups'=2,'blk'=4,'dp'=2,'sub'=2] {'blk','dp','sub'}, use_global_device_ids=true, to_apply=%region_7.8 | all-reduce | flops 1024 | bytes 8192 | tf_op jit(solution)/shard_map/psum | solution.py:58
  90.8 0.0 copy-start.2
  90.8 3.2 %fusion.1 = f32[2048]{0:T(1024)S(1)} fusion(bf16[1024,2048]{1,0:T(8,128)(2,1)} %copy-done, f32[1024]{0:T(1024)S(1)} %broadcast_divide_fusion.5), kind=kLoop, calls=%fused_computation.8 | loop fusion | flops 6289408 | bytes 4206592 | tf_op jit(solution)/shard_map/reduce_sum | solution.py:55
  94.0 3.1 %fusion.2 = f32[1024]{0:T(1024)S(1)} fusion(bf16[1024,2048]{1,0:T(8,128)(2,1)} %copy-done, f32[2048]{0:T(1024)S(1)} %broadcast_divide_fusion.1), kind=kLoop, calls=%fused_computation.9 | loop fusion | flops 6290432 | bytes 4206592 | tf_op jit(solution)/shard_map/reduce_sum | solution.py:56
  97.1 29.7 %psum.30 = f32[1024]{0:T(1024)S(1)} all-reduce(f32[1024]{0:T(1024)S(1)} %fusion.2), channel_id=1, replica_groups=mesh['groups'=2,'blk'=4,'dp'=2,'sub'=2] {'blk','dp','sub'}, use_global_device_ids=true, to_apply=%region_10.11 | all-reduce | flops 1024 | bytes 8192 | tf_op jit(solution)/shard_map/psum | solution.py:60
  126.8 3.1 %fusion.3 = f32[2048]{0:T(1024)S(1)} fusion(bf16[1024,2048]{1,0:T(8,128)(2,1)} %copy-done, f32[1024]{0:T(1024)S(1)} %broadcast_divide_fusion.4), kind=kLoop, calls=%fused_computation.10 | loop fusion | flops 6289408 | bytes 4206592 | tf_op jit(solution)/shard_map/reduce_sum | solution.py:55
  129.9 3.1 %fusion.4 = f32[1024]{0:T(1024)S(1)} fusion(bf16[1024,2048]{1,0:T(8,128)(2,1)} %copy-done, f32[2048]{0:T(1024)S(1)} %broadcast_divide_fusion), kind=kLoop, calls=%fused_computation.11 | loop fusion | flops 6290432 | bytes 4206592 | tf_op jit(solution)/shard_map/reduce_sum | solution.py:56
  132.9 0.0 copy-done.2
  132.9 7.3 %fusion.9 = (f32[1024]{0:T(1024)S(1)}, f32[1024,2048]{1,0:T(8,128)}) fusion(pred[128,8,16,128]{3,2,1,0:T(8,128)(4,1)S(1)} %bitcast.12, f32[2048]{0:T(1024)S(1)} %add_rsqrt_fusion, bf16[8192,256]{1,0:T(8,128)(2,1)} %param.7, s32[]{:T(128)S(6)} %select_n.14, bf16[1024,512]{1,0:T(8,128)(2,1)S(1)} %copy-done.2), kind=kOutput, calls=%fused_computation.18 | convolution fusion | flops 1083702272 | bytes 12070916 | tf_op jit(solution)/shard_map/rd,kd->rk/dot_general | solution.py:45
  140.2 30.0 %all-reduce = (f32[1024]{0:T(1024)S(1)}, f32[1024]{0:T(1024)S(1)}) all-reduce(f32[1024]{0:T(1024)S(1)} %fusion.4, f32[1024]{0:T(1024)S(1)} %get-tuple-element.6), channel_id=1, replica_groups=mesh['groups'=2,'blk'=4,'dp'=2,'sub'=2] {'blk','dp','sub'}, use_global_device_ids=true, to_apply=%region_13.14 | all-reduce | flops 2048 | bytes 16384 | tf_op jit(solution)/shard_map/psum | solution.py:60
  170.2 7.4 %fusion.8 = bf16[1024,2048]{1,0:T(8,128)(2,1)S(1)} fusion(bf16[1024,2048]{1,0:T(8,128)(2,1)} %copy-done, f32[1024,2048]{1,0:T(8,128)} %get-tuple-element.7, pred[128,8,16,128]{3,2,1,0:T(8,128)(4,1)S(1)} %bitcast.13, f32[1024]{0:T(1024)S(1)} %broadcast_divide_fusion.3, f32[2048]{0:T(1024)S(1)} %broadcast_divide_fusion, f32[1024]{0:T(1024)S(1)} %get-tuple-element.3), kind=kLoop, calls=%fused_computation.15 | loop fusion | flops 20971520 | bytes 18890752 | tf_op jit(solution)/shard_map/convert_element_type | solution.py:64
  177.6 0.0 copy-start.1
  177.7 1.9 copy-done.1
  179.6 3.6 %fusion.25 = f32[1024,256]{1,0:T(8,128)} fusion(bf16[1024,2048]{1,0:T(8,128)(2,1)S(1)} %fusion.8, f32[2048]{0:T(1024)S(1)} %add_rsqrt_fusion, bf16[8192,256]{1,0:T(8,128)(2,1)} %param.7, s32[]{:T(128)S(6)} %select_n.14), kind=kOutput, calls=%fused_computation.52 | convolution fusion | flops 1075314688 | bytes 6299652 | tf_op jit(solution)/shard_map/dot_general | solution.py:65
  183.1 0.0 reduce-scatter.2.cloned.1.call-update
  183.2 4.8 %fusion.13 = f32[2048,256]{1,0:T(8,128)} fusion(bf16[1024,2048]{1,0:T(8,128)(2,1)} %copy-done.1, bf16[1024,512]{1,0:T(8,128)(2,1)S(1)} %copy-done.2), kind=kOutput, calls=%fused_computation.25 | convolution fusion | flops 1073741824 | bytes 6815744 | tf_op jit(solution)/shard_map/rk,rd->kd/dot_general | solution.py:66
  188.0 49.9 %reduce-scatter.2.cloned.1.call-done = f32[64,256]{1,0:T(8,128)} async-done(((f32[1024,256]{1,0:T(8,128)}), f32[64,256]{1,0:T(8,128)}) %reduce-scatter.2.cloned.1.call-update) | async-done | bytes 65552 | tf_op jit(solution)/shard_map/reduce_scatter | solution.py:67
  (9 shorter events, 0.0 us)
Async XLA Ops:
  7.2 44.2 %all-gather.2.cloned.1.call-start = ((), (), s32[]{:S(2)}) async-start(), calls=%async_computation.1 | async-start | bytes 1114112 | tf_op jit(solution)/shard_map/all_gather | solution.py:31
  10.5 227.4 %reduce-scatter.2.cloned.1.call-start = ((), (), s32[]{:S(2)}) async-start(), calls=%async_computation.2 | async-start | bytes 1114112 | tf_op jit(solution)/shard_map/reduce_scatter | solution.py:67
  56.3 2.0 copy-start
  90.8 42.1 %copy-start.2 = (bf16[1024,512]{1,0:T(8,128)(2,1)S(1)}, bf16[1024,512]{1,0:T(8,128)(2,1)}, u32[]{:S(2)}) copy-start(bf16[1024,512]{1,0:T(8,128)(2,1)} %all-gather.2.cloned.1.call-done) | copy-start | bytes 3145732
  177.6 1.9 copy-start.1
Sparse Core Ops, SparseCore 0:
  10.7 40.6 all-gather.1
  183.3 54.6 reduce-scatter.1

commit v2 on v1

v2 whole, which is shorter than its diff:
```python
import functools
import math

import jax
import jax.numpy as jnp
from jax import lax
from jax.experimental import pallas as pl
from jax.experimental.pallas import tpu as pltpu
from jax.sharding import PartitionSpec as P

TILE = 128
ITERS = 3
SOFTMAX_TEMPER = 0.1
EPSILON = 0.05
LOG2E = math.log2(math.e)
CODE_GAIN = LOG2E / EPSILON
PRED_GAIN = LOG2E / SOFTMAX_TEMPER
OFF = -1e30
MESH = pl.DeviceIdType.MESH
F32 = jnp.float32
BF16 = jnp.bfloat16


def unit_rows(matrix):
    values = matrix.astype(F32)
    return (values * lax.rsqrt(jnp.sum(values * values, axis=1, keepdims=True) + 1e-06)).astype(
        BF16
    )


def down_rows(row):
    return jnp.broadcast_to(row, (TILE, TILE)).T


def across_lanes(block):
    return jnp.sum(block.T, axis=0, keepdims=True)


def fold(block):
    return jnp.sum(block.reshape(block.shape[0] // 8, 8, block.shape[1]), axis=0)


def kernel(
    n_blk,
    n_dp,
    hit_dev,
    cols,
    region_ref,
    mask_ref,
    view_a_ref,
    view_b_ref,
    protos_ref,
    gview_ref,
    gproto_ref,
    rows_a,
    rows_b,
    protos,
    code,
    pred,
    lanes,
    colacc,
    colinv,
    rowinv,
    norminv,
    plane_msg,
    line_msg,
    hits2,
    red,
    s_in,
    x_in,
    z_out,
    z_in,
    load_sem,
    agz_send,
    agz_recv,
    agx_send,
    agx_recv,
    ags_send,
    ags_recv,
    arp_send,
    arp_recv,
    arz_send,
    arz_recv,
    rss_send,
    rss_recv,
    rsx_send,
    rsx_recv,
    rsz_send,
    rsz_recv,
):
    z = lax.axis_index("blk")
    x = lax.axis_index("dp")
    c = lax.axis_index("sub")
    plane = 2 * n_dp
    q = x * 2 + c
    group_rows = plane * hit_dev
    pairs = n_blk * n_dp
    tiles = cols // TILE
    first_tile = (z * plane + q) * tiles
    width = protos.shape[1]
    CC = min(256, cols)
    ctiles = CC // TILE

    barrier = pltpu.get_barrier_semaphore()

    def plane_id(step):
        other = lax.rem(q + step, plane)
        return {"dp": lax.div(other, 2), "sub": lax.rem(other, 2)}

    def line_id(step):
        return {"blk": lax.rem(z + step, n_blk)}

    for step in range(1, plane):
        pl.semaphore_signal(barrier, inc=1, device_id=plane_id(step), device_id_type=MESH)
    for step in range(1, n_blk):
        pl.semaphore_signal(barrier, inc=1, device_id=line_id(step), device_id_type=MESH)

    load = pltpu.make_async_copy(protos_ref.at[pl.ds(q * cols, cols)], protos, load_sem)
    load.start()
    rows_a[z, x, c] = unit_rows(view_a_ref[...])
    rows_b[z, x, c] = unit_rows(view_b_ref[...])
    pl.semaphore_wait(barrier, plane - 1 + n_blk - 1)

    sends = []

    def send(src, dst, send_sem, recv_sem, device):
        copy = pltpu.make_async_remote_copy(
            src_ref=src,
            dst_ref=dst,
            send_sem=send_sem,
            recv_sem=recv_sem,
            device_id=device,
            device_id_type=MESH,
        )
        copy.start()
        sends.append(copy)
        return copy

    def arrive(dst, send_sem, recv_sem, device):
        pltpu.make_async_remote_copy(
            src_ref=dst,
            dst_ref=dst,
            send_sem=send_sem,
            recv_sem=recv_sem,
            device_id=device,
            device_id_type=MESH,
        ).wait_recv()

    sub_id = {"sub": 1 - c}

    def source(k):
        return lax.rem(z - k + n_blk, n_blk)

    def near(dx):
        return lax.rem(x - dx + n_dp, n_dp)

    def to_sub(v, rows, k, dx):
        ref = rows.at[source(k), near(dx), c]
        send(ref, ref, ags_send.at[v, k, dx], ags_recv.at[v, k, dx], sub_id)

    def gather_a(v, rows, k):
        ref = rows.at[source(k), x, c]
        if k == 0:
            for step in range(1, n_blk):
                send(ref, ref, agz_send.at[v, step], agz_recv.at[v, step], line_id(step))
        else:
            arrive(ref, agz_send.at[v, k], agz_recv.at[v, k], line_id(k))
        for dx in range(1, n_dp):
            send(
                ref,
                ref,
                agx_send.at[v, k, dx],
                agx_recv.at[v, k, dx],
                {"dp": lax.rem(x + dx, n_dp)},
            )
        to_sub(v, rows, k, 0)

    def gather_b(v, rows, k):
        for dx in range(1, n_dp):
            ref = rows.at[source(k), near(dx), c]
            arrive(
                ref,
                agx_send.at[v, k, dx],
                agx_recv.at[v, k, dx],
                {"dp": lax.rem(x + dx, n_dp)},
            )
            to_sub(v, rows, k, dx)

    def gather_c(v, rows, k):
        for dx in range(n_dp):
            ref = rows.at[source(k), near(dx), 1 - c]
            arrive(ref, ags_send.at[v, k, dx], ags_recv.at[v, k, dx], sub_id)

    def bias(pair, core, tile, gain):
        region = region_ref[pair * 2 + core]
        return jnp.where(mask_ref[region, first_tile + tile] > 0, -gain, OFF).astype(F32)

    def score(rows, zi, xs, count, col):
        left = rows[zi, pl.ds(xs, count)].reshape(count * 2 * hit_dev, width)
        right = protos[pl.ds(col, CC), :]
        return lax.dot_general(
            left, right, (((1,), (1,)), ((), ())), preferred_element_type=F32
        )

    PX = min(2, n_dp)

    def code_group(k):
        zi = source(k)

        def step(t, carry):
            xs = (t % (n_dp // PX)) * PX
            ci = t // (n_dp // PX)
            col = pl.multiple_of(ci * CC, CC)
            s = score(rows_a, zi, xs, PX, col)
            for j in range(ctiles):
                total = None
                lane = pl.ds(pl.multiple_of(col + j * TILE, TILE), TILE)
                for i in range(PX):
                    for core in range(2):
                        lo = (i * 2 + core) * hit_dev
                        piece = s[lo : lo + hit_dev, j * TILE : (j + 1) * TILE]
                        b = bias(zi * n_dp + xs + i, core, ci * ctiles + j, CODE_GAIN)
                        e = jnp.exp2(piece * CODE_GAIN + b).astype(BF16)
                        row = pl.multiple_of(zi * group_rows + xs * 2 * hit_dev + lo, hit_dev)
                        code[pl.ds(row, hit_dev), lane] = e
                        part = fold(e.astype(F32))
                        total = part if total is None else total + part
                colacc[:, lane] = colacc[:, lane] + total
            return carry

        lax.fori_loop(0, (n_dp // PX) * (cols // CC), step, 0)

    def pred_group(zi):
        def block(t, carry):
            xs = t * PX
            lanes[...] = jnp.zeros_like(lanes)

            def step(ci, inner):
                col = pl.multiple_of(ci * CC, CC)
                s = score(rows_b, zi, xs, PX, col)
                for i in range(PX):
                    for core in range(2):
                        lo = (i * 2 + core) * hit_dev
                        total = None
                        for j in range(ctiles):
                            piece = s[lo : lo + hit_dev, j * TILE : (j + 1) * TILE]
                            b = bias(zi * n_dp + xs + i, core, ci * ctiles + j, PRED_GAIN)
                            e = jnp.exp2(piece * PRED_GAIN + b)
                            row = pl.multiple_of(
                                zi * group_rows + xs * 2 * hit_dev + lo, hit_dev
                            )
                            lane = pl.ds(pl.multiple_of(col + j * TILE, TILE), TILE)
                            pred[pl.ds(row, hit_dev), lane] = e
                            total = e if total is None else total + e
                        lanes[lo : lo + hit_dev, :] = lanes[lo : lo + hit_dev, :] + total
                return inner

            lax.fori_loop(0, cols // CC, step, 0)
            for i in range(PX):
                norminv[pl.ds(zi * n_dp + xs + i, 1), :] = across_lanes(
                    lanes[i * TILE : (i + 1) * TILE, :]
                )
            return carry

        lax.fori_loop(0, n_dp // PX, block, 0)

    def close_columns():
        total = jnp.sum(colacc[...], axis=0, keepdims=True)
        colinv[...] = jnp.broadcast_to(1.0 / total, colinv.shape)

    def column_pass():
        colacc[...] = jnp.zeros_like(colacc)

        def step(p, carry):
            scale = down_rows(rowinv[pl.ds(p, 1), :])
            row = pl.ds(pl.multiple_of(p * TILE, TILE), TILE)
            for j in range(tiles):
                lane = slice(j * TILE, (j + 1) * TILE)
                colacc[:, lane] = colacc[:, lane] + fold(code[row, lane].astype(F32) * scale)
            return carry

        lax.fori_loop(0, pairs, step, 0)
        close_columns()

    def row_pass(sweep):
        def step(p, carry):
            row = pl.ds(pl.multiple_of(p * TILE, TILE), TILE)
            total = None
            for j in range(tiles):
                lane = slice(j * TILE, (j + 1) * TILE)
                part = code[row, lane].astype(F32) * colinv[0:1, lane]
                total = part if total is None else total + part
            plane_msg[sweep, q, pl.ds(p, 1), :] = across_lanes(total)
            return carry

        lax.fori_loop(0, pairs, step, 0)

    def reduce_start(sweep):
        size = 2 * pairs if sweep == ITERS - 1 else pairs
        mine = plane_msg.at[sweep, q, pl.ds(0, size)]
        for step in range(1, plane):
            send(mine, mine, arp_send.at[sweep, step], arp_recv.at[sweep, step], plane_id(step))

    def reduce_middle(sweep):
        size = 2 * pairs if sweep == ITERS - 1 else pairs
        for step in range(1, plane):
            other = plane_msg.at[sweep, lax.rem(q - step + plane, plane), pl.ds(0, size)]
            arrive(other, arp_send.at[sweep, step], arp_recv.at[sweep, step], plane_id(step))
        total = plane_msg[sweep, 0, 0:size, :]
        for other in range(1, plane):
            total = total + plane_msg[sweep, other, 0:size, :]
        line_msg[sweep, z, 0:size, :] = total
        mine = line_msg.at[sweep, z, pl.ds(0, size)]
        for step in range(1, n_blk):
            send(mine, mine, arz_send.at[sweep, step], arz_recv.at[sweep, step], line_id(step))

    def reduce_end(sweep):
        size = 2 * pairs if sweep == ITERS - 1 else pairs
        for step in range(1, n_blk):
            other = line_msg.at[sweep, source(step), pl.ds(0, size)]
            arrive(other, arz_send.at[sweep, step], arz_recv.at[sweep, step], line_id(step))
        total = line_msg[sweep, 0, 0:size, :]
        for other in range(1, n_blk):
            total = total + line_msg[sweep, other, 0:size, :]
        rowinv[...] = 1.0 / total[0:pairs]
        if sweep == ITERS - 1:
            norminv[...] = (1.0 / SOFTMAX_TEMPER) / total[pairs:size]

    gather_a(0, rows_a, 0)
    load.wait()
    NC = min(256, cols)

    def normalize(t, carry):
        at = pl.ds(pl.multiple_of(t * NC, NC), NC)
        protos[at, :] = unit_rows(protos[at, :])
        return carry

    lax.fori_loop(0, cols // NC, normalize, 0)
    colacc[...] = jnp.zeros_like(colacc)
    gather_b(0, rows_a, 0)
    for k in range(n_blk):
        if k + 1 < n_blk:
            gather_a(0, rows_a, k + 1)
        if k == n_blk - 1:
            gather_a(1, rows_b, 0)
        gather_c(0, rows_a, k)
        code_group(k)
        if k + 1 < n_blk:
            gather_b(0, rows_a, k + 1)
    close_columns()
    for k in range(1, n_blk):
        gather_a(1, rows_b, k)
        gather_b(1, rows_b, k - 1)
    row_pass(0)
    reduce_start(0)
    gather_b(1, rows_b, n_blk - 1)
    for k in range(n_blk):
        gather_c(1, rows_b, k)

    share = [n_blk * i // 4 for i in range(5)]
    part = 0
    for sweep in range(ITERS):
        if sweep > 0:
            column_pass()
            row_pass(sweep)
            if sweep == ITERS - 1:
                plane_msg[sweep, q, pairs : 2 * pairs, :] = norminv[...]
            reduce_start(sweep)
        if sweep < 2:
            for zi in range(share[part], share[part + 1]):
                pred_group(zi)
            part += 1
        reduce_middle(sweep)
        if sweep < 2:
            for zi in range(share[part], share[part + 1]):
                pred_group(zi)
            part += 1
        reduce_end(sweep)

    def grad_group(zi, slot):
        def rows_step(t, carry):
            p = zi * n_dp + t
            row = pl.ds(pl.multiple_of(p * TILE, TILE), TILE)
            scale = down_rows(rowinv[pl.ds(p, 1), :] * (1.0 / SOFTMAX_TEMPER))
            weight = down_rows(norminv[pl.ds(p, 1), :])
            for j in range(tiles):
                lane = slice(j * TILE, (j + 1) * TILE)
                codes = (code[row, lane].astype(F32) * scale) * colinv[0:1, lane]
                code[row, lane] = (pred[row, lane] * weight - codes).astype(BF16)
            return carry

        lax.fori_loop(0, n_dp, rows_step, 0)

        def dot_step(t, carry):
            xs = t * PX
            size = PX * 2 * hit_dev
            row = pl.multiple_of(zi * group_rows + xs * 2 * hit_dev, size)
            part = jnp.dot(code[pl.ds(row, size), :], protos[...], preferred_element_type=F32)
            for i in range(PX):
                for core in range(2):
                    lo = (i * 2 + core) * hit_dev
                    hits2[slot, core, xs + i] = part[lo : lo + hit_dev, :]
            return carry

        lax.fori_loop(0, n_dp // PX, dot_step, 0)

    SLOTS = hits2.shape[0]
    order = list(range(1, n_blk)) + [0]
    sub_sends = {}
    dp_sends = {}

    def drain(copies):
        for old in copies:
            old.wait_send()
            sends[:] = [copy for copy in sends if copy is not old]

    def scatter_start(i):
        k = order[i]
        slot = i % SLOTS
        if i >= SLOTS:
            drain([sub_sends[i - SLOTS]])
        grad_group(lax.rem(z + k, n_blk), slot)
        sub_sends[i] = send(
            hits2.at[slot, 1 - c], s_in.at[k], rss_send.at[k], rss_recv.at[k], sub_id
        )

    def scatter_sub(i):
        k = order[i]
        slot = i % SLOTS
        arrive(s_in.at[k], rss_send.at[k], rss_recv.at[k], sub_id)
        if i >= SLOTS:
            drain(dp_sends[i - SLOTS])
        red[slot] = hits2[slot, c] + s_in[k]
        dp_sends[i] = []
        for dx in range(1, n_dp):
            other = lax.rem(x + dx, n_dp)
            dp_sends[i].append(
                send(
                    red.at[slot, other],
                    x_in.at[k, dx - 1],
                    rsx_send.at[k, dx],
                    rsx_recv.at[k, dx],
                    {"dp": other},
                )
            )

    def scatter_dp(i):
        k = order[i]
        total = red[i % SLOTS, x]
        for dx in range(1, n_dp):
            other = lax.rem(x + dx, n_dp)
            arrive(x_in.at[k, dx - 1], rsx_send.at[k, dx], rsx_recv.at[k, dx], {"dp": other})
            total = total + x_in[k, dx - 1]
        z_out[k] = total
        if k > 0:
            send(z_out.at[k], z_in.at[k], rsz_send.at[k], rsz_recv.at[k], line_id(k))

    def proto_cols(t, carry):
        lane = pl.ds(pl.multiple_of(t * CC, CC), CC)
        total = None
        for zi in range(n_blk):
            left = code[zi * group_rows : (zi + 1) * group_rows, lane]
            right = rows_b[zi].reshape(group_rows, width)
            part = lax.dot_general(
                left, right, (((0,), (0,)), ((), ())), preferred_element_type=F32
            )
            total = part if total is None else total + part
        gproto_ref[lane, :] = total
        return carry

    for i in range(n_blk):
        scatter_start(i)
        if i >= 1:
            scatter_sub(i - 1)
        if i >= 2:
            scatter_dp(i - 2)
    scatter_sub(n_blk - 1)
    chunks = cols // CC
    half = chunks // 2
    lax.fori_loop(0, half, proto_cols, 0)
    for i in range(max(0, n_blk - 2), n_blk):
        scatter_dp(i)
    lax.fori_loop(half, chunks, proto_cols, 0)
    total = z_out[0]
    for k in range(1, n_blk):
        arrive(z_in.at[k], rsz_send.at[k], rsz_recv.at[k], line_id(k))
        total = total + z_in[k]
    gview_ref[...] = total
    for copy in sends:
        copy.wait_send()


def body(view_a, view_b, prototypes, tile_mask, tile_region):
    n_blk = lax.axis_size("blk")
    n_dp = lax.axis_size("dp")
    hit_dev, width = view_a.shape
    plane = 2 * n_dp
    cols = prototypes.shape[0] // plane
    pairs = n_blk * n_dp
    hits = pairs * 2 * hit_dev
    slots = n_blk if n_blk <= 4 else 2
    dma = pltpu.SemaphoreType.DMA
    vmem = pl.BlockSpec(memory_space=pltpu.VMEM)
    smem = pl.BlockSpec(memory_space=pltpu.SMEM)
    return pl.pallas_call(
        functools.partial(kernel, n_blk, n_dp, hit_dev, cols),
        out_shape=(
            jax.ShapeDtypeStruct((hit_dev, width), F32),
            jax.ShapeDtypeStruct((cols, width), F32),
        ),
        in_specs=[smem, smem, vmem, vmem, pl.BlockSpec(memory_space=pl.ANY)],
        out_specs=(vmem, vmem),
        scratch_shapes=[
            pltpu.VMEM((n_blk, n_dp, 2, hit_dev, width), BF16),
            pltpu.VMEM((n_blk, n_dp, 2, hit_dev, width), BF16),
            pltpu.VMEM((cols, width), BF16),
            pltpu.VMEM((hits, cols), BF16),
            pltpu.VMEM((hits, cols), F32),
            pltpu.VMEM((min(2, n_dp) * 2 * hit_dev, TILE), F32),
            pltpu.VMEM((8, cols), F32),
            pltpu.VMEM((8, cols), F32),
            pltpu.VMEM((pairs, TILE), F32),
            pltpu.VMEM((pairs, TILE), F32),
            pltpu.VMEM((ITERS, plane, 2 * pairs, TILE), F32),
            pltpu.VMEM((ITERS, n_blk, 2 * pairs, TILE), F32),
            pltpu.VMEM((slots, 2, n_dp, hit_dev, width), F32),
            pltpu.VMEM((slots, n_dp, hit_dev, width), F32),
            pltpu.VMEM((n_blk, n_dp, hit_dev, width), F32),
            pltpu.VMEM((n_blk, n_dp - 1, hit_dev, width), F32),
            pltpu.VMEM((n_blk, hit_dev, width), F32),
            pltpu.VMEM((n_blk, hit_dev, width), F32),
            dma,
            dma((2, n_blk)),
            dma((2, n_blk)),
            dma((2, n_blk, n_dp)),
            dma((2, n_blk, n_dp)),
            dma((2, n_blk, n_dp)),
            dma((2, n_blk, n_dp)),
            dma((ITERS, plane)),
            dma((ITERS, plane)),
            dma((ITERS, n_blk)),
            dma((ITERS, n_blk)),
            dma((n_blk,)),
            dma((n_blk,)),
            dma((n_blk, n_dp)),
            dma((n_blk, n_dp)),
            dma((n_blk,)),
            dma((n_blk,)),
        ],
        compiler_params=pltpu.CompilerParams(
            collective_id=0, has_side_effects=True, vmem_limit_bytes=62 << 20
        ),
    )(tile_region, tile_mask, view_a, view_b, prototypes)


def solution(mesh):
    spread = P(("groups", "blk", "dp", "sub"), None)
    return jax.shard_map(
        body,
        mesh=mesh,
        in_specs=(spread, spread, P("blk", None), P(), P("groups")),
        out_specs=(spread, spread),
        check_vma=False,
    )
```

time: 245 us -> 73.7 us (0.30)
  blocking collectives: 91.2 us -> 0 us
  waiting for transfers between devices: 88.3 us -> 0 us
  Pallas kernels: 0 us -> 68.3 us
  other arithmetic: 25.6 us -> 0 us
  matrix products: 20.9 us -> 0 us
  between operations: 14.2 us -> 0.64 us
    psum x3 -> x0, blocking collectives: 91.2 us -> none  [the longest x2 59.6 us: body(): part = lax.psum(part, PART)]
    pallas_call x0 -> x1, Pallas kernels: none -> 68.3 us  [body(): pl.pallas_call(functools.partial(kernel, n_blk, n_dp, hit_dev, cols), out...]
    reduce_scatter x1 -> x0, waiting for transfers between devices: 49.9 us -> none  [body(): lax.psum_scatter(hit_part, PART, scatter_dimension=0, tiled=True)]
    all_gather x1 -> x0, waiting for transfers between devices: 38.3 us -> none  [body(): both = lax.all_gather(both, PART, axis=0, tiled=True)]
    dot_general x5 -> x0, matrix products: 20.9 us -> none  [the longest x2 11.6 us: scores(): jnp.einsum('rd,kd->rk', rows, protos, preferred_element_type=jnp.float32)]
    reduce_sum x8 -> x0, other arithmetic: 16.6 us -> none  [the longest x3 7.06 us: body(): part = jnp.sum(code * col[None, :], axis=1)]
    convert_element_type x2 -> x0, other arithmetic: 8.3 us -> none  [the longest x1 7.44 us: body(): grad = ((pred / norm[:, None] - row[:, None] * code * col[None, :]) / SOF...]
  transfers between devices with their start and end apart: 2 -> 0, of which waited for: 2 -> 0; matrix products, arithmetic and copies ran while one was open for 3% -> 0% of each run, Pallas kernels for 0% -> 0%
where the time goes in v2:
time: 73.7 us; the launch traced here: 73.5 us
  Pallas kernels  68.3 us (93%)
  local copies, waits for them, and re-layouts  4.52 us (6%)
    pallas_call x1, Pallas kernels, body(): pl.pallas_call(functools.partial(kernel, n_blk, n_dp, hit_dev, cols), out...  68.3 us
    unnamed x2, local copies, waits for them, and re-layouts  4.52 us

profile of v2, /device:TPU:0, one launch (start us, length us, event | category | flops | bytes accessed | tf_op | source)
XLA Modules:
  0.0 73.5 jit_solution(2444385620292412529)
XLA Ops:
  0.6 68.3 %shard_map.68 = (f32[64,256]{1,0:T(8,128)}, f32[2048,256]{1,0:T(8,128)}) custom-call(s32[16]{0:T(128)} %region_ref.1, s32[16,256]{1,0:T(8,128)} %mask_ref.1, bf16[64,256]{1,0:T(8,128)(2,1)} %view_a_ref.1, bf16[64,256]{1,0:T(8,128)(2,1)} %view_b_ref.1, bf16[8192,256]{1,0:T(8,128)(2,1)} %protos_ref.1), custom_call_target="tpu_custom_call" | custom-call | tf_op jit(solution)/shard_map/pallas_call | solution.py:505
  69.0 1.5 %copy.9 = f32[64,256]{1,0:T(8,128)} copy(f32[64,256]{1,0:T(8,128)} %get-tuple-element.4) | data formatting | bytes 131072
  70.4 3.0 %copy.10 = f32[2048,256]{1,0:T(8,128)} copy(f32[2048,256]{1,0:T(8,128)} %get-tuple-element.5) | data formatting | bytes 4194304

commit v3 on v2

--- a/solution.py
+++ b/solution.py
@@ -98,7 +98,7 @@
     tiles = cols // TILE
     first_tile = (z * plane + q) * tiles
     width = protos.shape[1]
-    CC = min(256, cols)
+    CC = min(1024, cols)
     ctiles = CC // TILE
 
     barrier = pltpu.get_barrier_semaphore()
@@ -110,16 +110,31 @@
     def line_id(step):
         return {"blk": lax.rem(z + step, n_blk)}
 
-    for step in range(1, plane):
-        pl.semaphore_signal(barrier, inc=1, device_id=plane_id(step), device_id_type=MESH)
-    for step in range(1, n_blk):
-        pl.semaphore_signal(barrier, inc=1, device_id=line_id(step), device_id_type=MESH)
+    direct = n_blk * plane <= 16
+    team = n_blk * plane if direct else plane
+    me = z * plane + q if direct else q
+
+    def team_id(step):
+        if not direct:
+            return plane_id(step)
+        other = lax.rem(me + step, team)
+        return {
+            "blk": lax.div(other, plane),
+            "dp": lax.rem(lax.div(other, 2), n_dp),
+            "sub": lax.rem(other, 2),
+        }
+
+    for step in range(1, team):
+        pl.semaphore_signal(barrier, inc=1, device_id=team_id(step), device_id_type=MESH)
+    if not direct:
+        for step in range(1, n_blk):
+            pl.semaphore_signal(barrier, inc=1, device_id=line_id(step), device_id_type=MESH)
 
     load = pltpu.make_async_copy(protos_ref.at[pl.ds(q * cols, cols)], protos, load_sem)
     load.start()
     rows_a[z, x, c] = unit_rows(view_a_ref[...])
     rows_b[z, x, c] = unit_rows(view_b_ref[...])
-    pl.semaphore_wait(barrier, plane - 1 + n_blk - 1)
+    pl.semaphore_wait(barrier, team - 1 + (0 if direct else n_blk - 1))
 
     sends = []
 
@@ -290,31 +305,41 @@
                 lane = slice(j * TILE, (j + 1) * TILE)
                 part = code[row, lane].astype(F32) * colinv[0:1, lane]
                 total = part if total is None else total + part
-            plane_msg[sweep, q, pl.ds(p, 1), :] = across_lanes(total)
+            plane_msg[sweep, me, pl.ds(p, 1), :] = across_lanes(total)
             return carry
 
         lax.fori_loop(0, pairs, step, 0)
 
     def reduce_start(sweep):
         size = 2 * pairs if sweep == ITERS - 1 else pairs
-        mine = plane_msg.at[sweep, q, pl.ds(0, size)]
-        for step in range(1, plane):
-            send(mine, mine, arp_send.at[sweep, step], arp_recv.at[sweep, step], plane_id(step))
+        mine = plane_msg.at[sweep, me, pl.ds(0, size)]
+        for step in range(1, team):
+            send(mine, mine, arp_send.at[sweep, step], arp_recv.at[sweep, step], team_id(step))
+
+    def close_rows(sweep, total):
+        rowinv[...] = 1.0 / total[0:pairs]
+        if sweep == ITERS - 1:
+            norminv[...] = (1.0 / SOFTMAX_TEMPER) / total[pairs : 2 * pairs]
 
     def reduce_middle(sweep):
         size = 2 * pairs if sweep == ITERS - 1 else pairs
-        for step in range(1, plane):
-            other = plane_msg.at[sweep, lax.rem(q - step + plane, plane), pl.ds(0, size)]
-            arrive(other, arp_send.at[sweep, step], arp_recv.at[sweep, step], plane_id(step))
+        for step in range(1, team):
+            other = plane_msg.at[sweep, lax.rem(me - step + team, team), pl.ds(0, size)]
+            arrive(other, arp_send.at[sweep, step], arp_recv.at[sweep, step], team_id(step))
         total = plane_msg[sweep, 0, 0:size, :]
-        for other in range(1, plane):
+        for other in range(1, team):
             total = total + plane_msg[sweep, other, 0:size, :]
+        if direct:
+            close_rows(sweep, total)
+            return
         line_msg[sweep, z, 0:size, :] = total
         mine = line_msg.at[sweep, z, pl.ds(0, size)]
         for step in range(1, n_blk):
             send(mine, mine, arz_send.at[sweep, step], arz_recv.at[sweep, step], line_id(step))
 
     def reduce_end(sweep):
+        if direct:
+            return
         size = 2 * pairs if sweep == ITERS - 1 else pairs
         for step in range(1, n_blk):
             other = line_msg.at[sweep, source(step), pl.ds(0, size)]
@@ -322,9 +347,7 @@
         total = line_msg[sweep, 0, 0:size, :]
         for other in range(1, n_blk):
             total = total + line_msg[sweep, other, 0:size, :]
-        rowinv[...] = 1.0 / total[0:pairs]
-        if sweep == ITERS - 1:
-            norminv[...] = (1.0 / SOFTMAX_TEMPER) / total[pairs:size]
+        close_rows(sweep, total)
 
     gather_a(0, rows_a, 0)
     load.wait()
@@ -358,13 +381,15 @@
         gather_c(1, rows_b, k)
 
     share = [n_blk * i // 4 for i in range(5)]
+    if direct:
+        share = [0, n_blk // 2, n_blk // 2, n_blk, n_blk]
     part = 0
     for sweep in range(ITERS):
         if sweep > 0:
             column_pass()
             row_pass(sweep)
             if sweep == ITERS - 1:
-                plane_msg[sweep, q, pairs : 2 * pairs, :] = norminv[...]
+                plane_msg[sweep, me, pairs : 2 * pairs, :] = norminv[...]
             reduce_start(sweep)
         if sweep < 2:
             for zi in range(share[part], share[part + 1]):
@@ -498,6 +523,7 @@
     cols = prototypes.shape[0] // plane
     pairs = n_blk * n_dp
     hits = pairs * 2 * hit_dev
+    team = n_blk * plane if n_blk * plane <= 16 else plane
     slots = n_blk if n_blk <= 4 else 2
     dma = pltpu.SemaphoreType.DMA
     vmem = pl.BlockSpec(memory_space=pltpu.VMEM)
@@ -521,7 +547,7 @@
             pltpu.VMEM((8, cols), F32),
             pltpu.VMEM((pairs, TILE), F32),
             pltpu.VMEM((pairs, TILE), F32),
-            pltpu.VMEM((ITERS, plane, 2 * pairs, TILE), F32),
+            pltpu.VMEM((ITERS, team, 2 * pairs, TILE), F32),
             pltpu.VMEM((ITERS, n_blk, 2 * pairs, TILE), F32),
             pltpu.VMEM((slots, 2, n_dp, hit_dev, width), F32),
             pltpu.VMEM((slots, n_dp, hit_dev, width), F32),
@@ -536,8 +562,8 @@
             dma((2, n_blk, n_dp)),
             dma((2, n_blk, n_dp)),
             dma((2, n_blk, n_dp)),
-            dma((ITERS, plane)),
-            dma((ITERS, plane)),
+            dma((ITERS, team)),
+            dma((ITERS, team)),
             dma((ITERS, n_blk)),
             dma((ITERS, n_blk)),
             dma((n_blk,)),
@@ -548,7 +574,7 @@
             dma((n_blk,)),
         ],
         compiler_params=pltpu.CompilerParams(
-            collective_id=0, has_side_effects=True, vmem_limit_bytes=62 << 20
+            collective_id=0, has_side_effects=True, vmem_limit_bytes=(50 if team > plane else 62) << 20
         ),
     )(tile_region, tile_mask, view_a, view_b, prototypes)
 

time: 73.7 us -> 67.9 us (0.921)
  Pallas kernels: 68.3 us -> 62.1 us
    pallas_call x1, Pallas kernels: 68.3 us -> 62.1 us  [body(): pl.pallas_call(functools.partial(kernel, n_blk, n_dp, hit_dev, cols), out...]
    unnamed x2 -> x10, local copies, waits for them, and re-layouts: 4.52 us -> 4.83 us
where the time goes in v3:
time: 67.9 us; the launch traced here: 67.6 us
  Pallas kernels  62.1 us (91%)
  local copies, waits for them, and re-layouts  4.83 us (7%)
    pallas_call x1, Pallas kernels, body(): pl.pallas_call(functools.partial(kernel, n_blk, n_dp, hit_dev, cols), out...  62.1 us
    unnamed x10, local copies, waits for them, and re-layouts  4.83 us

profile of v3, /device:TPU:0, one launch (start us, length us, event | category | flops | bytes accessed | tf_op | source)
XLA Modules:
  0.0 67.6 jit_solution(2077467142365580962)
XLA Ops:
  0.6 0.0 copy-start
  0.6 0.7 %copy-done = bf16[64,256]{1,0:T(8,128)(2,1)S(1)} copy-done((bf16[64,256]{1,0:T(8,128)(2,1)S(1)}, bf16[64,256]{1,0:T(8,128)(2,1)}, u32[]{:S(2)}) %copy-start) | copy-done | bytes 32792
  1.4 0.0 copy-start.1
  1.4 0.8 %copy-done.1 = bf16[64,256]{1,0:T(8,128)(2,1)S(1)} copy-done((bf16[64,256]{1,0:T(8,128)(2,1)S(1)}, bf16[64,256]{1,0:T(8,128)(2,1)}, u32[]{:S(2)}) %copy-start.1) | copy-done | bytes 32792
  2.1 0.0 copy-start.2
  2.2 0.7 %copy-done.2 = s32[16,256]{1,0:T(8,128)S(1)} copy-done((s32[16,256]{1,0:T(8,128)S(1)}, s32[16,256]{1,0:T(8,128)}, u32[]{:S(2)}) %copy-start.2) | copy-done | bytes 16408
  2.9 0.0 copy-start.3
  2.9 0.7 copy-done.3
  3.5 62.1 %shard_map.68 = (f32[64,256]{1,0:T(8,128)S(1)}, f32[2048,256]{1,0:T(8,128)S(1)}) custom-call(s32[16]{0:T(128)S(1)} %copy-done.3, s32[16,256]{1,0:T(8,128)S(1)} %copy-done.2, bf16[64,256]{1,0:T(8,128)(2,1)S(1)} %copy-done, bf16[64,256]{1,0:T(8,128)(2,1)S(1)} %copy-done.1, bf16[8192,256]{1,0:T(8,128)(2,1)} %protos_ref.1), custom_call_target="tpu_custom_call" | custom-call | tf_op jit(solution)/shard_map/pallas_call | solution.py:531
  65.6 0.6 copy.9
  66.3 1.3 %copy.10 = f32[2048,256]{1,0:T(8,128)} copy(f32[2048,256]{1,0:T(8,128)S(1)} %get-tuple-element.5) | data formatting | bytes 4194304
Async XLA Ops:
  0.6 0.8 %copy-start = (bf16[64,256]{1,0:T(8,128)(2,1)S(1)}, bf16[64,256]{1,0:T(8,128)(2,1)}, u32[]{:S(2)}) copy-start(bf16[64,256]{1,0:T(8,128)(2,1)} %view_a_ref.1) | copy-start | bytes 98308
  1.4 0.8 %copy-start.1 = (bf16[64,256]{1,0:T(8,128)(2,1)S(1)}, bf16[64,256]{1,0:T(8,128)(2,1)}, u32[]{:S(2)}) copy-start(bf16[64,256]{1,0:T(8,128)(2,1)} %view_b_ref.1) | copy-start | bytes 98308
  2.1 0.7 %copy-start.2 = (s32[16,256]{1,0:T(8,128)S(1)}, s32[16,256]{1,0:T(8,128)}, u32[]{:S(2)}) copy-start(s32[16,256]{1,0:T(8,128)} %mask_ref.1) | copy-start | bytes 49156
  2.9 0.7 copy-start.3

commit v4 on v3

--- a/solution.py
+++ b/solution.py
@@ -480,8 +480,10 @@
         if k > 0:
             send(z_out.at[k], z_in.at[k], rsz_send.at[k], rsz_recv.at[k], line_id(k))
 
+    PC = min(512, cols)
+
     def proto_cols(t, carry):
-        lane = pl.ds(pl.multiple_of(t * CC, CC), CC)
+        lane = pl.ds(pl.multiple_of(t * PC, PC), PC)
         total = None
         for zi in range(n_blk):
             left = code[zi * group_rows : (zi + 1) * group_rows, lane]
@@ -499,13 +501,15 @@
             scatter_sub(i - 1)
         if i >= 2:
             scatter_dp(i - 2)
+    chunks = cols // PC
+    cut = [chunks * i // 4 for i in range(5)]
+    lax.fori_loop(cut[0], cut[1], proto_cols, 0)
     scatter_sub(n_blk - 1)
-    chunks = cols // CC
-    half = chunks // 2
-    lax.fori_loop(0, half, proto_cols, 0)
-    for i in range(max(0, n_blk - 2), n_blk):
-        scatter_dp(i)
-    lax.fori_loop(half, chunks, proto_cols, 0)
+    if n_blk >= 2:
+        scatter_dp(n_blk - 2)
+    lax.fori_loop(cut[1], cut[2], proto_cols, 0)
+    scatter_dp(n_blk - 1)
+    lax.fori_loop(cut[2], cut[4], proto_cols, 0)
     total = z_out[0]
     for k in range(1, n_blk):
         arrive(z_in.at[k], rsz_send.at[k], rsz_recv.at[k], line_id(k))

time: 67.9 us -> 67.5 us (level)
  no operation moved by 1% of the time
where the time goes in v4:
time: 67.5 us; the launch traced here: 67.2 us
  Pallas kernels  61.7 us (91%)
  local copies, waits for them, and re-layouts  4.83 us (7%)
    pallas_call x1, Pallas kernels, body(): pl.pallas_call(functools.partial(kernel, n_blk, n_dp, hit_dev, cols), out...  61.7 us
    unnamed x10, local copies, waits for them, and re-layouts  4.83 us

profile of v4, /device:TPU:0, one launch (start us, length us, event | category | flops | bytes accessed | tf_op | source)
XLA Modules:
  0.0 67.2 jit_solution(6817087783336856247)
XLA Ops:
  0.6 0.0 copy-start
  0.6 0.7 %copy-done = bf16[64,256]{1,0:T(8,128)(2,1)S(1)} copy-done((bf16[64,256]{1,0:T(8,128)(2,1)S(1)}, bf16[64,256]{1,0:T(8,128)(2,1)}, u32[]{:S(2)}) %copy-start) | copy-done | bytes 32792
  1.4 0.0 copy-start.1
  1.4 0.8 %copy-done.1 = bf16[64,256]{1,0:T(8,128)(2,1)S(1)} copy-done((bf16[64,256]{1,0:T(8,128)(2,1)S(1)}, bf16[64,256]{1,0:T(8,128)(2,1)}, u32[]{:S(2)}) %copy-start.1) | copy-done | bytes 32792
  2.1 0.0 copy-start.2
  2.2 0.7 %copy-done.2 = s32[16,256]{1,0:T(8,128)S(1)} copy-done((s32[16,256]{1,0:T(8,128)S(1)}, s32[16,256]{1,0:T(8,128)}, u32[]{:S(2)}) %copy-start.2) | copy-done | bytes 16408
  2.9 0.0 copy-start.3
  2.9 0.7 copy-done.3
  3.5 61.7 %shard_map.68 = (f32[64,256]{1,0:T(8,128)S(1)}, f32[2048,256]{1,0:T(8,128)S(1)}) custom-call(s32[16]{0:T(128)S(1)} %copy-done.3, s32[16,256]{1,0:T(8,128)S(1)} %copy-done.2, bf16[64,256]{1,0:T(8,128)(2,1)S(1)} %copy-done, bf16[64,256]{1,0:T(8,128)(2,1)S(1)} %copy-done.1, bf16[8192,256]{1,0:T(8,128)(2,1)} %protos_ref.1), custom_call_target="tpu_custom_call" | custom-call | tf_op jit(solution)/shard_map/pallas_call | solution.py:535
  65.3 0.6 copy.9
  65.9 1.3 %copy.10 = f32[2048,256]{1,0:T(8,128)} copy(f32[2048,256]{1,0:T(8,128)S(1)} %get-tuple-element.5) | data formatting | bytes 4194304
Async XLA Ops:
  0.6 0.8 %copy-start = (bf16[64,256]{1,0:T(8,128)(2,1)S(1)}, bf16[64,256]{1,0:T(8,128)(2,1)}, u32[]{:S(2)}) copy-start(bf16[64,256]{1,0:T(8,128)(2,1)} %view_a_ref.1) | copy-start | bytes 98308
  1.4 0.8 %copy-start.1 = (bf16[64,256]{1,0:T(8,128)(2,1)S(1)}, bf16[64,256]{1,0:T(8,128)(2,1)}, u32[]{:S(2)}) copy-start(bf16[64,256]{1,0:T(8,128)(2,1)} %view_b_ref.1) | copy-start | bytes 98308
  2.1 0.7 %copy-start.2 = (s32[16,256]{1,0:T(8,128)S(1)}, s32[16,256]{1,0:T(8,128)}, u32[]{:S(2)}) copy-start(s32[16,256]{1,0:T(8,128)} %mask_ref.1) | copy-start | bytes 49156
  2.9 0.7 copy-start.3
